TPU v7x, 32 devices: a whole 2x2x4 slice. The times are simulated.
32 devices in a mesh: groups: 2 (over x), frame: 16 (over z, y, core).
Axes of the slice: x: 2, y: 2, z: 4, core: 2. Of those that a mesh axis runs over, the one named last changes fastest.
Arguments:
- queries: bfloat16 [16384, 2560], P(('groups', 'frame')), parts along dimension 0, may hold values from -48 to 48, as said below
- keys_values: bfloat16 [16384, 2, 2560], P(('groups', 'frame')), parts along dimension 0, may hold values from -6 to 6, as said below
- offsets: int32 [128, 3], P(('groups', 'frame')), parts along dimension 0, may hold values from -2 to 2, as said below
- ref_owner: int32 [8], P('groups'), parts along dimension 0, may hold values from 0 to 15
- ref_slot: int32 [8], P('groups'), parts along dimension 0, may hold values from 0 to 2
Outputs:
- attended: bfloat16 [16384, 2560], P(('groups', 'frame')), parts along dimension 0
There are 2 independent parts, one for each index of `groups`. A program takes and returns all parts, laid end to end along the dimension named above; each array names one. Nothing has to cross between parts.
Inputs may be any that keep to these rules, and one draw needn't show every extreme that they name: `queries`: custom draw; aside from the table's range nothing further. `keys_values`: custom draw. `offsets`: each row holds 3 different nonzero numbers.
All inputs are finite; a program needn't handle non-finite values.
Results may differ from a plain program's by a relative error of at most 0.0047.
Values may be sent and summed in bfloat16 or wider, within the bound.
No kernel may reach another device: no remote copies, remote signals or barrier semaphores. Data moves between devices by JAX's collectives and lax.ppermute only.
A program may use at most 128 MiB of HBM per device.

v0:
```python
import math

import jax
import jax.numpy as jnp
from jax import lax
from jax.sharding import PartitionSpec as P

DH = 128
BLK = 128
WIN = 3
REACH = 2
NREF = 4
REFLEN = 256


def extended(cells, sides, width):
    for axis, dim in sides:
        count = lax.axis_size(axis)
        ends = count - 1
        head = lax.slice_in_dim(cells, 0, width, axis=dim)
        tail = lax.slice_in_dim(cells, cells.shape[dim] - width, cells.shape[dim], axis=dim)
        cells = jnp.concatenate(
            [
                lax.ppermute(tail, axis, [(i, (i + 1) % count) for i in range(ends)]),
                cells,
                lax.ppermute(head, axis, [((i + 1) % count, i) for i in range(ends)]),
            ],
            axis=dim,
        )
    return cells


def broadcast(value, axis, source):
    kept = jnp.where(lax.axis_index(axis) == source, value, 0).astype(value.dtype)
    return lax.psum(kept, axis)


def on_device(queries, keys_values, offsets, ref_owner, ref_slot):
    tok_rows = queries.shape[0]
    columns = queries.shape[1]
    head_count = columns // DH
    block_count = tok_rows // BLK
    group_heads = math.gcd(head_count, 4)
    groups = head_count // group_heads
    group_width = group_heads * DH
    score_scale = 1.0 / math.sqrt(DH)
    device_index = lax.axis_index("frame")
    frames_total = lax.axis_size("frame")
    margin = REACH * BLK
    padded = extended(keys_values, (("frame", 0),), margin)
    received = []
    for slot_id in range(NREF):
        own_block = lax.dynamic_slice_in_dim(keys_values, ref_slot[slot_id] * BLK, REFLEN, 0)
        received.append(broadcast(own_block, "frame", ref_owner[slot_id]))
    ref_pairs = jnp.concatenate(received, 0)
    block_pairs = padded.reshape(block_count + 2 * REACH, BLK, 2, columns)
    block_offsets = jnp.concatenate([jnp.zeros((block_count, 1), jnp.int32), offsets], 1)
    global_block = device_index * block_count + jnp.arange(block_count, dtype=jnp.int32)
    target = global_block[:, None] + block_offsets
    usable = (target >= 0) & (target < frames_total * block_count)
    key_mask = jnp.repeat(usable, BLK, axis=1)
    local_index = jnp.arange(block_count, dtype=jnp.int32)[:, None] + REACH + block_offsets

    def one_group(group_id):
        query_group = lax.dynamic_slice_in_dim(
            queries, group_id * group_width, group_width, 1
        ).reshape(block_count, BLK, group_heads, DH)
        pair_group = lax.dynamic_slice_in_dim(block_pairs, group_id * group_width, group_width, 3)
        window_pairs = jnp.take(pair_group, local_index, axis=0).reshape(
            block_count, (1 + WIN) * BLK, 2, group_heads, DH
        )
        ref_group = lax.dynamic_slice_in_dim(
            ref_pairs, group_id * group_width, group_width, 2
        ).reshape(NREF * REFLEN, 2, group_heads, DH)
        window_scores = (
            jnp.einsum(
                "bqhd,bkhd->bhqk",
                query_group,
                window_pairs[:, :, 0],
                preferred_element_type=jnp.float32,
            )
            * score_scale
        )
        window_scores = jnp.where(key_mask[:, None, None, :], window_scores, -jnp.inf)
        ref_scores = (
            jnp.einsum(
                "bqhd,khd->bhqk", query_group, ref_group[:, 0], preferred_element_type=jnp.float32
            )
            * score_scale
        )
        row_max = jnp.maximum(jnp.max(window_scores, -1), jnp.max(ref_scores, -1))
        window_probs = jnp.exp(window_scores - row_max[..., None])
        ref_probs = jnp.exp(ref_scores - row_max[..., None])
        totals = jnp.sum(window_probs, -1) + jnp.sum(ref_probs, -1)
        weighted = jnp.einsum(
            "bhqk,bkhd->bqhd",
            window_probs.astype(jnp.bfloat16),
            window_pairs[:, :, 1],
            preferred_element_type=jnp.float32,
        )
        weighted = weighted + jnp.einsum(
            "bhqk,khd->bqhd",
            ref_probs.astype(jnp.bfloat16),
            ref_group[:, 1],
            preferred_element_type=jnp.float32,
        )
        result = weighted / jnp.transpose(totals, (0, 2, 1))[..., None]
        return result.astype(jnp.bfloat16).reshape(tok_rows, group_width)

    stacked = lax.map(one_group, jnp.arange(groups, dtype=jnp.int32))
    return jnp.transpose(stacked, (1, 0, 2)).reshape(tok_rows, columns)


def solution(mesh):
    placed = (
        P(("groups", "frame"), None),
        P(("groups", "frame"), None, None),
        P(("groups", "frame"), None),
        P("groups"),
        P("groups"),
    )
    return jax.shard_map(
        on_device,
        mesh=mesh,
        in_specs=placed,
        out_specs=P(("groups", "frame"), None),
        check_vma=False,
    )
```

profile of v0, /device:TPU:0, one launch (start us, length us, event | category | flops | bytes accessed | tf_op | source)
XLA Modules:
  0.0 501.7 jit_solution(7052127736287008784)
XLA Ops:
  10.5 16.5 %constant_dynamic-slice_fusion.6 = (bf16[256,2,2560]{2,1,0:T(2,128)(2,1)}, bf16[256,2,2560]{2,1,0:T(2,128)(2,1)}, bf16[256,2,2560]{2,1,0:T(2,128)(2,1)}, bf16[25...) fusion(bf16[512,2,2560]{2,1,0:T(2,128)(2,1)} %param.8, s32[]{:T(128)S(6)} %select_n.69, ...), kind=kLoop, calls=%fused_computation.60 | loop fusion | bytes 31457296 | tf_op jit(solution)/shard_map/dynamic_slice | solution.py:53
  28.3 4.5 collective-permute-start
  32.8 5.8 %copy.74 = bf16[256,2,2560]{0,2,1:T(8,128)(2,1)S(1)} copy(bf16[256,2,2560]{2,1,0:T(2,128)(2,1)} %get-tuple-element.98) | data formatting | bytes 5242880
  39.2 7.3 %copy.73 = bf16[256,2,2560]{0,2,1:T(8,128)(2,1)} copy(bf16[256,2,2560]{2,1,0:T(2,128)(2,1)} %get-tuple-element.94) | data formatting | bytes 5242880
  47.8 2.6 broadcast_select_fusion
  50.4 5.8 %copy.72 = bf16[256,2,2560]{0,2,1:T(8,128)(2,1)S(1)} copy(bf16[256,2,2560]{2,1,0:T(2,128)(2,1)} %get-tuple-element.95) | data formatting | bytes 5242880
  56.8 7.4 %copy.71 = bf16[256,2,2560]{0,2,1:T(8,128)(2,1)} copy(bf16[256,2,2560]{2,1,0:T(2,128)(2,1)} %get-tuple-element.93) | data formatting | bytes 5242880
  64.8 2.7 broadcast_select_fusion.2
  68.4 17.2 %pad_maximum_fusion = bf16[1024,2,2560]{2,1,0:T(2,128)(2,1)} fusion(bf16[256,2,2560]{2,1,0:T(2,128)(2,1)} %collective-permute-done.1, bf16[512,2,2560]{2,1,0:T(2,128)(2,1)} %param.8, bf16[256,2,2560]{2,1,0:T(2,128)(2,1)} %collective-permute-done), kind=kLoop, calls=%fused_computation.49 | loop fusion | flops 10485760 | bytes 20971520 | tf_op jit(solution)/shard_map/concatenate | solution.py:22
  85.6 186.7 %all-reduce.4.cloned.1.call-done = (bf16[256,2,2560]{0,2,1:T(8,128)(2,1)}, bf16[256,2,2560]{0,2,1:T(8,128)(2,1)}, bf16[256,2,2560]{0,2,1:T(8,128)(2,1)}, bf16[256,2,2560]{0,2,1:T(8,128)(2,1)}) async-done(((bf16[256,2,2560]{0,2,1:T(8,128)(2,1)}, bf16[256,2,2560]{0,2,1:T(8,128)(2,1)}, bf16[256,2,2560]{0,2,1:T(8,128)(2,1)}, bf16[256,2,2560]{0,2,1:T(8,128)(2,1)}), (bf16[256,2,2560]{0,2,1:T(8,128)(2,1)}, ...) | async-done | bytes 10485776 | tf_op jit(solution)/shard_map/psum | solution.py:35
  272.2 10.0 %pad_maximum_fusion.1 = bf16[1024,2,2560]{0,2,1:T(8,128)(2,1)} fusion(bf16[256,2,2560]{0,2,1:T(8,128)(2,1)} %get-tuple-element.83, bf16[256,2,2560]{0,2,1:T(8,128)(2,1)} %get-tuple-element.84, bf16[256,2,2560]{0,2,1:T(8,128)(2,1)} %get-tuple-element.85, bf16[256,2,2560]{0,2,1:T(8,128)(2,1)} %get-tuple-element.86), kind=kLoop, calls=%fused_computation.50 | loop fusion | flops 41943040 | bytes 20971520 | tf_op jit(solution)/shard_map/concatenate | solution.py:55
  282.2 208.2 %while.11 = (s32[]{:T(128)}, bf16[5,512,512]{1,2,0:T(8,128)(2,1)}, s32[4,4]{1,0:T(4,128)S(1)}, s32[5]{0:T(128)S(1)}, bf16[8,128,2,2560]{3,2,1,0:T(2,128)(2,1)}, ...) while((s32[]{:T(128)}, bf16[5,512,512]{1,2,0:T(8,128)(2,1)}, ...), condition=%wide.region_9.10_spmd.clone, body=%wide.region_4.9_spmd.clone.sunk | while | flops 1637610624 | bytes 128607016 | solution.py:110
  284.7 1.8 constant_dynamic-slice_fusion.11
  286.5 4.6 bitcast_reduce_fusion.2
  291.1 3.0 constant_dynamic-slice_fusion.12
  294.3 9.9 %gather_fusion = bf16[16,128,2,512]{3,2,1,0:T(2,128)(2,1)} fusion(bf16[8,128,2,512]{3,2,1,0:T(2,128)(2,1)S(1)} %constant_dynamic-slice_fusion.12, s32[1024]{0:T(1024)S(1)} %pad_clamp_fusion.2), kind=kCustom, calls=%fused_computation.clone.clone.1 | custom fusion | bytes 8388672 | tf_op jit(solution)/shard_map/while/body/eval_jaxpr/jit(_take)/gather | solution.py:69
  304.2 7.6 %reshape.95 = bf16[4,512,2,4,128]{4,3,2,1,0:T(4,128)(2,1)} reshape(bf16[16,128,2,512]{3,2,1,0:T(2,128)(2,1)} %gather_fusion) | data formatting | bytes 8388608 | tf_op jit(solution)/shard_map/while/body/eval_jaxpr/jit(_take)/gather | solution.py:69
  312.0 3.0 copy_select_fusion.2
  320.6 1.8 divide_convert_fusion.2
  326.3 1.8 constant_dynamic-slice_fusion.11
  328.1 4.6 bitcast_reduce_fusion.2
  332.8 3.0 constant_dynamic-slice_fusion.12
  335.9 9.9 %gather_fusion = bf16[16,128,2,512]{3,2,1,0:T(2,128)(2,1)} fusion(bf16[8,128,2,512]{3,2,1,0:T(2,128)(2,1)S(1)} %constant_dynamic-slice_fusion.12, s32[1024]{0:T(1024)S(1)} %pad_clamp_fusion.2), kind=kCustom, calls=%fused_computation.clone.clone.1 | custom fusion | bytes 8388672 | tf_op jit(solution)/shard_map/while/body/eval_jaxpr/jit(_take)/gather | solution.py:69
  345.9 7.6 %reshape.95 = bf16[4,512,2,4,128]{4,3,2,1,0:T(4,128)(2,1)} reshape(bf16[16,128,2,512]{3,2,1,0:T(2,128)(2,1)} %gather_fusion) | data formatting | bytes 8388608 | tf_op jit(solution)/shard_map/while/body/eval_jaxpr/jit(_take)/gather | solution.py:69
  353.6 3.0 copy_select_fusion.2
  362.2 1.8 divide_convert_fusion.2
  368.0 1.8 constant_dynamic-slice_fusion.11
  369.8 4.6 bitcast_reduce_fusion.2
  374.4 3.0 constant_dynamic-slice_fusion.12
  377.6 9.9 %gather_fusion = bf16[16,128,2,512]{3,2,1,0:T(2,128)(2,1)} fusion(bf16[8,128,2,512]{3,2,1,0:T(2,128)(2,1)S(1)} %constant_dynamic-slice_fusion.12, s32[1024]{0:T(1024)S(1)} %pad_clamp_fusion.2), kind=kCustom, calls=%fused_computation.clone.clone.1 | custom fusion | bytes 8388672 | tf_op jit(solution)/shard_map/while/body/eval_jaxpr/jit(_take)/gather | solution.py:69
  387.5 7.6 %reshape.95 = bf16[4,512,2,4,128]{4,3,2,1,0:T(4,128)(2,1)} reshape(bf16[16,128,2,512]{3,2,1,0:T(2,128)(2,1)} %gather_fusion) | data formatting | bytes 8388608 | tf_op jit(solution)/shard_map/while/body/eval_jaxpr/jit(_take)/gather | solution.py:69
  395.3 3.0 copy_select_fusion.2
  403.9 1.8 divide_convert_fusion.2
  409.6 1.8 constant_dynamic-slice_fusion.11
  411.4 4.6 bitcast_reduce_fusion.2
  416.1 3.0 constant_dynamic-slice_fusion.12
  419.2 9.9 %gather_fusion = bf16[16,128,2,512]{3,2,1,0:T(2,128)(2,1)} fusion(bf16[8,128,2,512]{3,2,1,0:T(2,128)(2,1)S(1)} %constant_dynamic-slice_fusion.12, s32[1024]{0:T(1024)S(1)} %pad_clamp_fusion.2), kind=kCustom, calls=%fused_computation.clone.clone.1 | custom fusion | bytes 8388672 | tf_op jit(solution)/shard_map/while/body/eval_jaxpr/jit(_take)/gather | solution.py:69
  429.2 7.6 %reshape.95 = bf16[4,512,2,4,128]{4,3,2,1,0:T(4,128)(2,1)} reshape(bf16[16,128,2,512]{3,2,1,0:T(2,128)(2,1)} %gather_fusion) | data formatting | bytes 8388608 | tf_op jit(solution)/shard_map/while/body/eval_jaxpr/jit(_take)/gather | solution.py:69
  436.9 3.0 copy_select_fusion.2
  445.5 1.8 divide_convert_fusion.2
  451.2 1.8 constant_dynamic-slice_fusion.11
  453.0 4.6 bitcast_reduce_fusion.2
  457.7 3.0 constant_dynamic-slice_fusion.12
  460.8 9.9 %gather_fusion = bf16[16,128,2,512]{3,2,1,0:T(2,128)(2,1)} fusion(bf16[8,128,2,512]{3,2,1,0:T(2,128)(2,1)S(1)} %constant_dynamic-slice_fusion.12, s32[1024]{0:T(1024)S(1)} %pad_clamp_fusion.2), kind=kCustom, calls=%fused_computation.clone.clone.1 | custom fusion | bytes 8388672 | tf_op jit(solution)/shard_map/while/body/eval_jaxpr/jit(_take)/gather | solution.py:69
  470.8 7.6 %reshape.95 = bf16[4,512,2,4,128]{4,3,2,1,0:T(4,128)(2,1)} reshape(bf16[16,128,2,512]{3,2,1,0:T(2,128)(2,1)} %gather_fusion) | data formatting | bytes 8388608 | tf_op jit(solution)/shard_map/while/body/eval_jaxpr/jit(_take)/gather | solution.py:69
  478.5 3.0 copy_select_fusion.2
  487.1 1.8 divide_convert_fusion.2
  490.4 4.4 copy.61
  (167 shorter events, 49.5 us)
Async XLA Ops:
  6.5 265.7 %all-reduce.4.cloned.1.call-start = ((), (), s32[]{:S(2)}) async-start(), calls=%async_computation | async-start | bytes 20971520 | tf_op jit(solution)/shard_map/psum | solution.py:35
  27.0 11.6 %copy-start.3 = (s32[4]{0:T(128)S(1)}, s32[4]{0:T(128)}, u32[]{:S(2)}) copy-start(s32[4]{0:T(128)} %param.10) | copy-start | bytes 52
  27.0 41.3 %collective-permute-start.1 = (bf16[256,2,2560]{2,1,0:T(2,128)(2,1)}, bf16[256,2,2560]{2,1,0:T(2,128)(2,1)}, u32[]{:S(2)}, u32[]{:S(2)}) collective-permute-start(bf16[256,2,2560]{2,1,0:T(2,128)(2,1)} %get-tuple-element.96), channel_id=1, source_target_pairs={{1,0},{2,1},{3,2},{4,3},{5,4},{6,5},{7,6},{8,7},{9,8},{10,9},{11,1... | collective-permute-start | bytes 7864328 | tf_op jit(solution)/shard_map/ppermute | solution.py:26
  28.3 40.1 %collective-permute-start = (bf16[256,2,2560]{2,1,0:T(2,128)(2,1)}, bf16[256,2,2560]{2,1,0:T(2,128)(2,1)}, u32[]{:S(2)}, u32[]{:S(2)}) collective-permute-start(bf16[256,2,2560]{2,1,0:T(2,128)(2,1)} %get-tuple-element.97), channel_id=1, source_target_pairs={{0,1},{1,2},{2,3},{3,4},{4,5},{5,6},{6,7},{7,8},{8,9},{9,10},{10,1... | collective-permute-start | bytes 7864328 | tf_op jit(solution)/shard_map/ppermute | solution.py:24
  67.5 0.7 copy-start.2
  286.4 4.6 copy-start
  311.9 3.9 slice-start
  311.9 4.7 slice-start.1
  316.7 1.8 copy-start.1
  328.1 4.6 copy-start
  353.6 3.9 slice-start
  353.6 4.7 slice-start.1
  358.3 1.8 copy-start.1
  369.8 4.6 copy-start
  395.2 3.9 slice-start
  395.3 4.7 slice-start.1
  400.0 1.8 copy-start.1
  411.4 4.6 copy-start
  436.9 3.9 slice-start
  436.9 4.7 slice-start.1
  441.6 1.8 copy-start.1
  453.0 4.6 copy-start
  478.5 3.9 slice-start
  478.5 4.7 slice-start.1
  483.2 1.8 copy-start.1
Sparse Core Ops, SparseCore 0:
  67.7 204.5 all-reduce.3
where the time goes:
time: 504 us; the launch traced here: 502 us
  waiting for transfers between devices  187 us (37%)
  local copies, waits for them, and re-layouts  183 us (36%)
  other arithmetic  63.7 us (13%)
  matrix products  39.7 us (8%)
  between operations  18.5 us (4%)
  starting transfers between devices  5.79 us (1%)
    psum x1, waiting for transfers between devices, broadcast(): return lax.psum(kept, axis)  187 us
    gather x10, local copies, waits for them, and re-layouts, one_group(): jnp.take(pair_group, local_index, axis=0)  87.9 us
    unnamed x8, local copies, waits for them, and re-layouts  26.9 us
    dot_general x5, matrix products, one_group(): jnp.einsum('bqhd,khd->bhqk', query_group, ref_group[:, 0], preferred_elem...  22.9 us
    concatenate x1, other arithmetic, extended(): jnp.concatenate([lax.ppermute(tail, axis, [(i, (i + 1) % count) for i in...  17.2 us
    dynamic_slice x1, local copies, waits for them, and re-layouts, on_device(): lax.dynamic_slice_in_dim(keys_values, ref_slot[slot_id] * BLK, REFLEN, 0)  16.5 us
    reduce_sum x10, other arithmetic, one_group(): totals = jnp.sum(window_probs, -1) + jnp.sum(ref_probs, -1)  15.6 us
    select_n x10, other arithmetic, one_group(): jnp.take(pair_group, local_index, axis=0)  15.2 us
  transfers between devices with their start and end apart: 3, of which 1 were waited for; matrix products, arithmetic and copies ran while one was open for 10% of the time, Pallas kernels for 0%

commit v1 on v0

v1 whole, which is shorter than its diff:
```python
import functools
import math

import jax
import jax.numpy as jnp
from jax import lax
from jax.experimental import pallas as pl
from jax.experimental.pallas import tpu as pltpu
from jax.sharding import PartitionSpec as P

DH = 128
BLK = 128
WIN = 3
REACH = 2
NREF = 4
REFLEN = 256
SCALE = math.log2(math.e) / math.sqrt(DH)
MASKED = -1e30


def cost(flops, moved, exps):
    return pl.CostEstimate(flops=flops, bytes_accessed=moved, transcendentals=exps)


def split_kernel(core_ref, kv_ref, mine_ref, theirs_ref):
    half = mine_ref.shape[2]
    core = core_ref[0]
    for out_ref, side in ((mine_ref, core), (theirs_ref, 1 - core)):
        start = pl.multiple_of(side * half, DH)
        for which in range(2):
            out_ref[which] = kv_ref[:, which, pl.ds(start, half)]


def split_columns(core, keys_values):
    rows, _, columns = keys_values.shape
    half = columns // 2
    step = 64
    out_spec = pl.BlockSpec((2, step, half), lambda i, c: (0, i, 0))
    return pl.pallas_call(
        split_kernel,
        out_shape=[jax.ShapeDtypeStruct((2, rows, half), keys_values.dtype)] * 2,
        grid_spec=pltpu.PrefetchScalarGridSpec(
            num_scalar_prefetch=1,
            grid=(rows // step,),
            in_specs=[pl.BlockSpec((step, 2, columns), lambda i, c: (i, 0, 0))],
            out_specs=[out_spec] * 2,
        ),
        cost_estimate=cost(0, 4 * rows * columns * 2, 0),
        name="split_columns",
    )(core, keys_values)


def attend(query, keys, values, biases, state):
    scores = []
    for key, bias in zip(keys, biases):
        s = lax.dot_general(
            key, query, (((1,), (1,)), ((), ())), preferred_element_type=jnp.float32
        )
        scores.append(s if bias is None else s + bias)
    top = functools.reduce(jnp.maximum, [jnp.max(s, 0, keepdims=True) for s in scores])
    if state is not None:
        old_top, old_total, old_sum = state
        top = jnp.maximum(top, old_top)
    total = None
    summed = None
    for s, value in zip(scores, values):
        probs = jnp.exp2((s - top) * SCALE)
        part = jnp.sum(probs, 0, keepdims=True)
        total = part if total is None else total + part
        part = lax.dot_general(
            value,
            probs.astype(jnp.bfloat16),
            (((0,), (0,)), ((), ())),
            preferred_element_type=jnp.float32,
        )
        summed = part if summed is None else summed + part
    if state is not None:
        fade = jnp.exp2((old_top - top) * SCALE)
        total = total + fade * old_total
        summed = summed + fade * old_sum
    return top, total, summed


def window_kernel(table, qm_ref, qo_ref, mine, other, left, right, sum_ref, top_ref, total_ref, ext):
    rows = mine.shape[1]
    margin = left.shape[1]
    core = table[0]
    blocks = rows // BLK
    for which in range(2):
        ext[which, 0:margin] = left[which]
        ext[which, pl.ds(pl.multiple_of(margin + core * rows, BLK), rows)] = mine[which]
        ext[which, pl.ds(pl.multiple_of(margin + (1 - core) * rows, BLK), rows)] = other[which]
        ext[which, margin + 2 * rows : 2 * margin + 2 * rows] = right[which]
    count = 2 * blocks * (1 + WIN)
    for block in range(2 * blocks):
        q_ref = qm_ref if block < blocks else qo_ref
        at = (block % blocks) * BLK
        query = q_ref[at : at + BLK, :]
        keys, values, biases = [], [], []
        for listed in range(1 + WIN):
            entry = 1 + block * (1 + WIN) + listed
            start = pl.multiple_of(table[entry] * BLK, BLK)
            keys.append(ext[0, pl.ds(start, BLK), :])
            values.append(ext[1, pl.ds(start, BLK), :])
            usable = table[count + entry]
            biases.append(None if listed == 0 else jnp.where(usable == 1, 0.0, MASKED))
        top, total, summed = attend(query, keys, values, biases, None)
        lanes = slice(block * BLK, (block + 1) * BLK)
        sum_ref[:, lanes] = summed
        top_ref[0, :, lanes] = top
        total_ref[0, :, lanes] = total


def window_part(table, queries, q_other, mine, other, left, right):
    rows, half = q_other.shape
    heads = half // DH
    margin = left.shape[1]
    lanes = 2 * rows
    head = lambda h, t: (0, h)
    head3 = lambda h, t: (0, 0, h)
    state = lambda h, t: (h, 0, 0)
    keys = 2 * rows * (1 + WIN) * BLK
    return pl.pallas_call(
        window_kernel,
        out_shape=[
            jax.ShapeDtypeStruct((half, lanes), jnp.float32),
            jax.ShapeDtypeStruct((heads, 1, lanes), jnp.float32),
            jax.ShapeDtypeStruct((heads, 1, lanes), jnp.float32),
        ],
        grid_spec=pltpu.PrefetchScalarGridSpec(
            num_scalar_prefetch=1,
            grid=(heads,),
            in_specs=[
                pl.BlockSpec((rows, DH), lambda h, t: (0, t[0] * heads + h)),
                pl.BlockSpec((rows, DH), head),
                pl.BlockSpec((2, rows, DH), head3),
                pl.BlockSpec((2, rows, DH), head3),
                pl.BlockSpec((2, margin, DH), head3),
                pl.BlockSpec((2, margin, DH), head3),
            ],
            out_specs=[
                pl.BlockSpec((DH, lanes), lambda h, t: (h, 0)),
                pl.BlockSpec((1, 1, lanes), state),
                pl.BlockSpec((1, 1, lanes), state),
            ],
            scratch_shapes=[pltpu.VMEM((2, 2 * rows + 2 * margin, DH), mine.dtype)],
        ),
        cost_estimate=cost(
            4 * keys * DH * heads, half * (lanes * 6 + 8 * (rows + margin)), keys * heads
        ),
        name="window_part",
    )(table, queries, q_other, mine, other, left, right)


def ref_kernel(count, chunk, core_ref, qm_ref, qo_ref, *refs):
    pieces = refs[:count]
    sum_in, top_in, total_in, sum_ref, top_ref, total_ref = refs[count:]
    rows = qm_ref.shape[0]
    keys = [piece[0] for piece in pieces]
    values = [piece[1] for piece in pieces]
    for part in range(2 * rows // chunk):
        lanes = slice(part * chunk, (part + 1) * chunk)
        q_ref = qm_ref if part * chunk < rows else qo_ref
        at = (part * chunk) % rows
        state = (top_in[0, :, lanes], total_in[0, :, lanes], sum_in[:, lanes])
        top, total, summed = attend(
            q_ref[at : at + chunk, :], keys, values, [None] * count, state
        )
        sum_ref[:, lanes] = summed
        top_ref[0, :, lanes] = top
        total_ref[0, :, lanes] = total


def ref_part(core, queries, q_other, pieces, state):
    rows, half = q_other.shape
    heads = half // DH
    lanes = 2 * rows
    head3 = lambda h, c: (0, 0, h)
    at_head = lambda h, c: (h, 0, 0)
    state_specs = [
        pl.BlockSpec((DH, lanes), lambda h, c: (h, 0)),
        pl.BlockSpec((1, 1, lanes), at_head),
        pl.BlockSpec((1, 1, lanes), at_head),
    ]
    listed = sum(piece.shape[1] for piece in pieces)
    count = len(pieces)
    return pl.pallas_call(
        functools.partial(ref_kernel, count, 2 * BLK),
        out_shape=[jax.ShapeDtypeStruct(s.shape, s.dtype) for s in state],
        grid_spec=pltpu.PrefetchScalarGridSpec(
            num_scalar_prefetch=1,
            grid=(heads,),
            in_specs=[
                pl.BlockSpec((rows, DH), lambda h, c: (0, c[0] * heads + h)),
                pl.BlockSpec((rows, DH), lambda h, c: (0, h)),
            ]
            + [pl.BlockSpec((2, piece.shape[1], DH), head3) for piece in pieces]
            + state_specs,
            out_specs=state_specs,
        ),
        input_output_aliases={3 + count + i: i for i in range(3)},
        cost_estimate=cost(
            4 * lanes * listed * half, half * (lanes * 10 + 4 * listed), lanes * listed * heads
        ),
        name="ref_part",
    )(core, queries, q_other, *pieces, *state)


def last_kernel(count, chunk, core_ref, q_ref, *refs):
    pieces = refs[:count]
    sum_in, top_in, total_in, out_ref = refs[count:]
    keys = [piece[0] for piece in pieces]
    values = [piece[1] for piece in pieces]
    for part in range(q_ref.shape[0] // chunk):
        lanes = slice(part * chunk, (part + 1) * chunk)
        state = (top_in[0, :, lanes], total_in[0, :, lanes], sum_in[:, lanes])
        _, total, summed = attend(q_ref[lanes, :], keys, values, [None] * count, state)
        result = summed * (1.0 / total)
        out_ref[lanes, :] = jnp.transpose(result).astype(out_ref.dtype)


def last_part(core, query, own, pieces, state):
    rows = query.shape[0]
    half = state[0].shape[0]
    heads = half // DH
    head3 = lambda h, c: (0, 0, h)
    side = 0 if own else 1
    at_head = lambda h, c: (h, 0, side)
    column = (lambda h, c: (0, c[0] * heads + h)) if own else (lambda h, c: (0, h))
    listed = sum(piece.shape[1] for piece in pieces)
    count = len(pieces)
    return pl.pallas_call(
        functools.partial(last_kernel, count, 2 * BLK),
        out_shape=jax.ShapeDtypeStruct(query.shape, query.dtype),
        grid_spec=pltpu.PrefetchScalarGridSpec(
            num_scalar_prefetch=1,
            grid=(heads,),
            in_specs=[pl.BlockSpec((rows, DH), column)]
            + [pl.BlockSpec((2, piece.shape[1], DH), head3) for piece in pieces]
            + [
                pl.BlockSpec((DH, rows), lambda h, c: (h, side)),
                pl.BlockSpec((1, 1, rows), at_head),
                pl.BlockSpec((1, 1, rows), at_head),
            ],
            out_specs=pl.BlockSpec((rows, DH), column),
        ),
        cost_estimate=cost(
            4 * rows * listed * half, half * (rows * 8 + 4 * listed), rows * listed * heads
        ),
        name="last_own" if own else "last_other",
    )(core, query, *pieces, *state)


def join_kernel(core_ref, got_ref, _, out_ref):
    out_ref[...] = got_ref[...]


def join_columns(core, got, partial):
    rows, half = got.shape
    step = 128
    return pl.pallas_call(
        join_kernel,
        out_shape=jax.ShapeDtypeStruct(partial.shape, partial.dtype),
        grid_spec=pltpu.PrefetchScalarGridSpec(
            num_scalar_prefetch=1,
            grid=(rows // step,),
            in_specs=[
                pl.BlockSpec((step, half), lambda i, c: (i, 0)),
                pl.BlockSpec(memory_space=pl.ANY),
            ],
            out_specs=pl.BlockSpec((step, half), lambda i, c: (i, 1 - c[0])),
        ),
        input_output_aliases={2: 0},
        cost_estimate=cost(0, 4 * rows * half, 0),
        name="join_columns",
    )(core, got, partial)


def on_device(queries, keys_values, offsets, ref_owner, ref_slot):
    rows, columns = queries.shape
    half = columns // 2
    blocks = rows // BLK
    margin = REACH * BLK
    frames = lax.axis_size("frame")
    me = lax.axis_index("frame")
    core = me % 2
    partner = me + 1 - 2 * core
    chips = frames // 2
    chip = me // 2
    core_arg = core.reshape(1).astype(jnp.int32)
    swap = [(i, i ^ 1) for i in range(frames)]

    mine, theirs = split_columns(core_arg, keys_values)
    other = lax.ppermute(theirs, "frame", swap)
    q_other = lax.ppermute(
        lax.dynamic_slice_in_dim(queries, (1 - core) * half, half, 1), "frame", swap
    )
    offsets_other = lax.ppermute(offsets, "frame", swap)

    order = list(range(0, chips, 2)) + list(range(chips - 1 - chips % 2, 0, -2))
    place = jnp.where(chip % 2 == 0, chip // 2, chips - 1 - chip // 2)
    owner_chip = ref_owner // 2
    owner_place = jnp.where(owner_chip % 2 == 0, owner_chip // 2, chips - 1 - owner_chip // 2)

    def ring(step):
        return [
            (2 * order[i] + c, 2 * order[(i + step) % chips] + c)
            for c in range(2)
            for i in range(chips)
        ]

    up, down = ring(1), ring(-1)
    reach = chips // 2
    piece_rows = NREF * REFLEN // chips
    per_ref = REFLEN // piece_rows
    cut = piece_rows // 2

    def held(piece, low, size):
        piece = piece % chips
        ref = piece // per_ref
        start = ref_slot[ref] * BLK + (piece % per_ref) * piece_rows + low
        own = lax.dynamic_slice_in_dim(mine, start, size, 1)
        near = lax.dynamic_slice_in_dim(other, start, size, 1)
        return ref_owner[ref] == me, ref_owner[ref] == partner, own, near

    def offer(piece, low, size):
        _, is_near, own, near = held(piece, low, size)
        return jnp.where(is_near, near, own)

    def merge(piece, low, size, got):
        is_own, is_near, own, near = held(piece, low, size)
        return jnp.where(is_own, own, jnp.where(is_near, near, got))

    send_up = offer(place + reach, 0, cut)
    send_down = offer(place + reach, cut, cut)
    for step in range(reach):
        if step == 1:
            piece = place + reach - 1
            send_up = jnp.concatenate(
                [merge(piece, 0, cut, got_up), offer(piece, cut, cut)], 1
            )
            piece = place + reach + 1
            send_down = jnp.concatenate(
                [offer(piece, 0, cut), merge(piece, cut, cut, got_down)], 1
            )
        elif step > 1:
            send_up = merge(place + reach - step, 0, piece_rows, got_up)
            send_down = merge(place + reach + step, 0, piece_rows, got_down)
        got_up = lax.ppermute(send_up, "frame", up)
        got_down = lax.ppermute(send_down, "frame", down)
    away = (place - owner_place[place // per_ref]) % chips
    row = lax.broadcasted_iota(jnp.int32, (1, piece_rows, 1), 1)
    from_below = (away < reach) | ((away == reach) & (row < cut))
    own_piece = merge(place, 0, piece_rows, jnp.where(from_below, got_up, got_down))

    along = [(2 * i + c, 2 * i + 2 + c) for i in range(chips - 1) for c in range(2)]
    back = [(b, a) for a, b in along]
    tail = jnp.where(core == 1, mine[:, rows - margin :], other[:, rows - margin :])
    head = jnp.where(core == 0, mine[:, :margin], other[:, :margin])
    left = lax.ppermute(tail, "frame", along)
    right = lax.ppermute(head, "frame", back)

    first = jnp.stack([me, partner]) * blocks
    listed = jnp.concatenate(
        [jnp.zeros((2, blocks, 1), jnp.int32), jnp.stack([offsets, offsets_other])], 2
    )
    target = (first[:, None] + jnp.arange(blocks, dtype=jnp.int32))[:, :, None] + listed
    usable = (target >= 0) & (target < frames * blocks)
    table = jnp.concatenate(
        [
            core_arg,
            (target - chip * 2 * blocks + REACH).reshape(-1).astype(jnp.int32),
            usable.reshape(-1).astype(jnp.int32),
        ]
    )
    state = window_part(table, queries, q_other, mine, other, left, right)

    send_up = send_down = own_piece
    fresh = [own_piece]
    for step in range(reach):
        if step == reach - 1:
            send_up, send_down = send_up[:, :cut], send_down[:, cut:]
        send_up = lax.ppermute(send_up, "frame", up)
        send_down = lax.ppermute(send_down, "frame", down)
        fresh = fresh + [send_up, send_down]
        if step < reach - 1:
            state = ref_part(core_arg, queries, q_other, fresh, state)
            fresh = []

    out_other = last_part(core_arg, q_other, False, fresh, state)
    got = lax.ppermute(out_other, "frame", swap)
    out = last_part(core_arg, queries, True, fresh, state)
    return join_columns(core_arg, got, out)


def solution(mesh):
    placed = (
        P(("groups", "frame"), None),
        P(("groups", "frame"), None, None),
        P(("groups", "frame"), None),
        P("groups"),
        P("groups"),
    )
    return jax.shard_map(
        on_device,
        mesh=mesh,
        in_specs=placed,
        out_specs=P(("groups", "frame"), None),
        check_vma=False,
    )
```

time: 504 us -> 288 us (0.57)
  local copies, waits for them, and re-layouts: 183 us -> 5.73 us
  Pallas kernels: 0 us -> 101 us
  waiting for transfers between devices: 187 us -> 116 us
  other arithmetic: 63.7 us -> 21.4 us
  matrix products: 39.7 us -> 0 us
  starting transfers between devices: 5.79 us -> 26.3 us
    psum x1 -> x0, waiting for transfers between devices: 187 us -> none  [broadcast(): return lax.psum(kept, axis)]
    ppermute x2 -> x22, waiting for transfers between devices: 0.01 us -> 116 us  [the longest x4 57.1 us: on_device(): send_down = lax.ppermute(send_down, 'frame', down)]
    pallas_call x0 -> x8, Pallas kernels: none -> 101 us  [the longest x3 37.1 us: ref_part(): pl.pallas_call(functools.partial(ref_kernel, count, 2 * BLK), out_shape=[...]
    gather x10 -> x0, local copies, waits for them, and re-layouts: 87.9 us -> none  [one_group(): jnp.take(pair_group, local_index, axis=0)]
    dynamic_slice x21 -> x3, local copies, waits for them, and re-layouts: 48.8 us -> 2.49 us  [the longest x1 1.21 us: on_device(): lax.dynamic_slice_in_dim(queries, (1 - core) * half, half, 1)]
    dot_general x20 -> x0, matrix products: 39.7 us -> none  [the longest x5 22.9 us: one_group(): jnp.einsum('bqhd,khd->bhqk', query_group, ref_group[:, 0], preferred_elem...]
    unnamed x8 -> x30, local copies, waits for them, and re-layouts: 26.9 us -> 3.02 us
    concatenate x2 -> x3, other arithmetic: 27.2 us -> 3.38 us  [the longest x1 1.9 us: on_device(): jnp.concatenate([merge(piece, 0, cut, got_up), offer(piece, cut, cut)], 1)]
  transfers between devices with their start and end apart: 3 -> 22, of which waited for: 1 -> 11; matrix products, arithmetic and copies ran while one was open for 10% -> 5% of each run, Pallas kernels for 0% -> 26%
where the time goes in v1:
time: 288 us; the launch traced here: 286 us
  waiting for transfers between devices  116 us (40%)
  Pallas kernels  101 us (35%)
  starting transfers between devices  26.3 us (9%)
  other arithmetic  21.4 us (7%)
  between operations  15.2 us (5%)
  local copies, waits for them, and re-layouts  5.73 us (2%)
    ppermute x4, waiting for transfers between devices, on_device(): send_down = lax.ppermute(send_down, 'frame', down)  57.1 us
    pallas_call x3, Pallas kernels, ref_part(): pl.pallas_call(functools.partial(ref_kernel, count, 2 * BLK), out_shape=[...  37.1 us
    pallas_call x1, Pallas kernels, window_part(): pl.pallas_call(window_kernel, out_shape=[jax.ShapeDtypeStruct((half, lane...  28 us
    ppermute x4, waiting for transfers between devices, on_device(): got_up = lax.ppermute(send_up, 'frame', up)  23.6 us
    ppermute x4, waiting for transfers between devices, on_device(): got_down = lax.ppermute(send_down, 'frame', down)  22.1 us
    pallas_call x2, Pallas kernels, last_part(): pl.pallas_call(functools.partial(last_kernel, count, 2 * BLK), out_shape=...  19.1 us
    pallas_call x1, Pallas kernels, split_columns(): pl.pallas_call(split_kernel, out_shape=[jax.ShapeDtypeStruct((2, rows, ha...  13.6 us
    ppermute x4, waiting for transfers between devices, on_device(): send_up = lax.ppermute(send_up, 'frame', up)  13 us
  transfers between devices with their start and end apart: 22, of which 11 were waited for; matrix products, arithmetic and copies ran while one was open for 5% of the time, Pallas kernels for 26%

profile of v1, /device:TPU:0, one launch (start us, length us, event | category | flops | bytes accessed | tf_op | source)
XLA Modules:
  0.0 286.0 jit_solution(6503053776411620400)
XLA Ops:
  0.0 13.6 %split_columns.1 = (bf16[2,512,1280]{2,1,0:T(8,128)(2,1)}, bf16[2,512,1280]{2,1,0:T(8,128)(2,1)}) custom-call(s32[1]{0:T(128)} %bitcast.core_ref, bf16[512,2,2560]{2,1,0:T(2,128)(2,1)} %kv_ref.1), custom_call_target="tpu_custom_call" | custom-call | bytes 10485760 | tf_op jit(solution)/shard_map/split_columns/pallas_call | solution.py:39
  13.6 0.5 collective-permute-start.1
  14.1 0.7 fusion
  19.0 2.8 dynamic-slice_select_fusion.1
  21.8 2.9 %collective-permute-start.2 = (bf16[2,64,1280]{2,1,0:T(8,128)(2,1)}, bf16[2,64,1280]{2,1,0:T(8,128)(2,1)}, u32[]{:S(2)}, u32[]{:S(2)}) collective-permute-start(bf16[2,64,1280]{2,1,0:T(8,128)(2,1)} %get-tuple-element.40), channel_id=1, source_target_pairs={{0,4},{4,8},{8,12},{12,14},{14,10},{10,6},{6,2},{2,0},{1,5},{5,9},... | collective-permute-start | bytes 983048 | tf_op jit(solution)/shard_map/ppermute | solution.py:349
  26.1 6.9 %collective-permute-done.2 = bf16[2,64,1280]{2,1,0:T(8,128)(2,1)} collective-permute-done((bf16[2,64,1280]{2,1,0:T(8,128)(2,1)}, bf16[2,64,1280]{2,1,0:T(8,128)(2,1)}, u32[]{:S(2)}, u32[]{:S(2)}) %collective-permute-start.2) | collective-permute-done | bytes 327712 | tf_op jit(solution)/shard_map/ppermute | solution.py:349
  33.0 1.5 collective-permute-done.6
  34.5 2.2 select_select_fusion.5
  36.8 0.9 pad_maximum_fusion.1
  39.8 1.9 pad_maximum_fusion
  41.7 1.7 collective-permute-start.3
  43.4 10.2 %collective-permute-done.7 = bf16[2,128,1280]{2,1,0:T(8,128)(2,1)} collective-permute-done((bf16[2,128,1280]{2,1,0:T(8,128)(2,1)}, bf16[2,128,1280]{2,1,0:T(8,128)(2,1)}, u32[]{:S(2)}, u32[]{:S(2)}) %collective-permute-start.7) | collective-permute-done | bytes 655392 | tf_op jit(solution)/shard_map/ppermute | solution.py:350
  53.6 1.5 select_select_fusion.2
  55.1 0.6 collective-permute-start.8
  59.5 10.4 %collective-permute-done.8 = bf16[2,128,1280]{2,1,0:T(8,128)(2,1)} collective-permute-done((bf16[2,128,1280]{2,1,0:T(8,128)(2,1)S(1)}, bf16[2,128,1280]{2,1,0:T(8,128)(2,1)}, u32[]{:S(2)}, u32[]{:S(2)}) %collective-permute-start.8) | collective-permute-done | bytes 655392 | tf_op jit(solution)/shard_map/ppermute | solution.py:350
  69.9 3.3 %select_select_fusion.1 = (bf16[2,128,1280]{2,1,0:T(8,128)(2,1)}, bf16[2,128,1280]{2,1,0:T(8,128)(2,1)}) fusion(bf16[2,128,1280]{2,1,0:T(8,128)(2,1)} %collective-permute-done.8, bf16[2,512,1280]{2,1,0:T(8,128)(2,1)} %collective-permute-done.1.other, s32[]{:T(128)S(6)} %select_n.430, bf16[2,512,1280]{2,1,0:T(8,128)(2,1)S(1)} %copy-done.1, pred[]{:T(512)S(6)} %eq.104, ...), kind=kLoop, calls=%fused_computation.5 | loop fusion | flops 1310720 | bytes 5242892 | tf_op jit(solution)/shard_map/jit(_where)/select_n | solution.py:332
  73.2 1.7 collective-permute-start.4
  77.0 10.0 %collective-permute-done.4 = bf16[2,128,1280]{2,1,0:T(8,128)(2,1)} collective-permute-done((bf16[2,128,1280]{2,1,0:T(8,128)(2,1)}, bf16[2,128,1280]{2,1,0:T(8,128)(2,1)}, u32[]{:S(2)}, u32[]{:S(2)}) %collective-permute-start.4) | collective-permute-done | bytes 655392 | tf_op jit(solution)/shard_map/ppermute | solution.py:349
  87.0 2.6 select_select_fusion.3
  89.6 2.1 collective-permute-start.5
  91.7 1.2 constant_dynamic-slice_fusion
  92.9 0.5 collective-permute-start.18
  93.4 0.6 dynamic_slice.138
  96.5 6.6 %collective-permute-done.5 = bf16[2,128,1280]{2,1,0:T(8,128)(2,1)} collective-permute-done((bf16[2,128,1280]{2,1,0:T(8,128)(2,1)}, bf16[2,128,1280]{2,1,0:T(8,128)(2,1)}, u32[]{:S(2)}, u32[]{:S(2)}) %collective-permute-start.5) | collective-permute-done | bytes 655392 | tf_op jit(solution)/shard_map/ppermute | solution.py:349
  103.2 1.9 select_select_fusion.refs_0_
  105.1 2.0 collective-permute-start.10
  107.1 3.4 %slice_select_fusion = (bf16[2,256,1280]{2,1,0:T(8,128)(2,1)}, bf16[2,256,1280]{2,1,0:T(8,128)(2,1)}) fusion(bf16[2,512,1280]{2,1,0:T(8,128)(2,1)} %collective-permute-done.1.other, bf16[2,512,1280]{2,1,0:T(8,128)(2,1)S(1)} %copy-done.2, pred[]{:T(512)S(6)} %eq.110, pred[]{:T(512)S(6)} %eq.109), kind=kLoop, calls=%fused_computation | loop fusion | flops 1310720 | bytes 7864322 | tf_op jit(solution)/shard_map/jit(_where)/select_n | solution.py:359
  110.6 3.7 %collective-permute-start.19 = (bf16[2,256,1280]{2,1,0:T(8,128)(2,1)}, bf16[2,256,1280]{2,1,0:T(8,128)(2,1)S(1)}, u32[]{:S(2)}, u32[]{:S(2)}) collective-permute-start(bf16[2,256,1280]{2,1,0:T(8,128)(2,1)} %get-tuple-element.34), channel_id=1, source_target_pairs={{0,2},{1,3},{2,4},{3,5},{4,6},{5,7},{6,8},{7,9},{8,10},{9,11},{10,... | collective-permute-start | bytes 3932168 | tf_op jit(solution)/shard_map/ppermute | solution.py:360
  114.3 1.3 collective-permute-start.20
  115.6 5.6 %collective-permute-done.10.refs_1_ = bf16[2,128,1280]{2,1,0:T(8,128)(2,1)S(1)} collective-permute-done((bf16[2,128,1280]{2,1,0:T(8,128)(2,1)S(1)}, bf16[2,128,1280]{2,1,0:T(8,128)(2,1)S(1)}, u32[]{:S(2)}, u32[]{:S(2)}) %collective-permute-start.10) | collective-permute-done | bytes 655392 | tf_op jit(solution)/shard_map/ppermute | solution.py:383
  121.2 0.6 collective-permute-start.11
  121.8 28.1 %collective-permute-done.14.refs_2_ = bf16[2,128,1280]{2,1,0:T(8,128)(2,1)} collective-permute-done((bf16[2,128,1280]{2,1,0:T(8,128)(2,1)S(1)}, bf16[2,128,1280]{2,1,0:T(8,128)(2,1)}, u32[]{:S(2)}, u32[]{:S(2)}) %collective-permute-start.14) | collective-permute-done | bytes 655392 | tf_op jit(solution)/shard_map/ppermute | solution.py:384
  149.9 3.0 %collective-permute-start.15 = (bf16[2,128,1280]{2,1,0:T(8,128)(2,1)}, bf16[2,128,1280]{2,1,0:T(8,128)(2,1)}, u32[]{:S(2)}, u32[]{:S(2)}) collective-permute-start(bf16[2,128,1280]{2,1,0:T(8,128)(2,1)} %collective-permute-done.14.refs_2_), channel_id=1, source_target_pairs={{0,2},{4,0},{8,4},{12,8},{14,12},{10,14},{6,10},{2,6},{1,3},{5,1},... | collective-permute-start | bytes 1966088 | tf_op jit(solution)/shard_map/ppermute | solution.py:384
  153.1 7.4 %collective-permute-done.11.refs_0_ = bf16[2,128,1280]{2,1,0:T(8,128)(2,1)S(1)} collective-permute-done((bf16[2,128,1280]{2,1,0:T(8,128)(2,1)S(1)}, bf16[2,128,1280]{2,1,0:T(8,128)(2,1)S(1)}, u32[]{:S(2)}, u32[]{:S(2)}) %collective-permute-start.11) | collective-permute-done | bytes 655392 | tf_op jit(solution)/shard_map/ppermute | solution.py:383
  160.5 29.0 %collective-permute-done.15.refs_1_ = bf16[2,128,1280]{2,1,0:T(8,128)(2,1)} collective-permute-done((bf16[2,128,1280]{2,1,0:T(8,128)(2,1)}, bf16[2,128,1280]{2,1,0:T(8,128)(2,1)}, u32[]{:S(2)}, u32[]{:S(2)}) %collective-permute-start.15) | collective-permute-done | bytes 655392 | tf_op jit(solution)/shard_map/ppermute | solution.py:384
  189.6 2.5 collective-permute-start.16
  192.4 0.6 pad_add_fusion.2.table
  193.0 1.0 copy-done.8
  194.0 28.0 %window_part.1 = (f32[1280,1024]{1,0:T(8,128)}, f32[10,1,1024]{2,1,0:T(1,128)}, f32[10,1,1024]{2,1,0:T(1,128)}) custom-call(s32[65]{0:T(128)} %pad_add_fusion.2.table, bf16[512,2560]{1,0:T(8,128)(2,1)} %q_ref.1, bf16[512,1280]{1,0:T(8,128)(2,1)} %collective-permute-done.qo_ref.q_ref, bf16[2,512,1280]{2,1,0:T(8,128)(2,1)} %get-tuple-element.19.mine, ...), custom_call_target="tpu_custom_call" | custom-call | flops 2684354560 | bytes 15728640 | tf_op jit(solution)/shard_map/window_part/pallas_call | solution.py:123
  222.2 2.2 collective-permute-start.17
  224.4 13.0 %ref_part.3 = (f32[1280,1024]{1,0:T(8,128)}, f32[10,1,1024]{2,1,0:T(1,128)}, f32[10,1,1024]{2,1,0:T(1,128)}) custom-call(s32[1]{0:T(128)} %bitcast.core_ref, bf16[512,2560]{1,0:T(8,128)(2,1)} %q_ref.1, bf16[512,1280]{1,0:T(8,128)(2,1)} %collective-permute-done.qo_ref.q_ref, ...), custom_call_target="tpu_custom_call", output_to_operand_aliasing={{0}: (6, {}), {1}: (7, {}), {2}: (8, {})} | custom-call | flops 2013265920 | bytes 15073280 | tf_op jit(solution)/shard_map/ref_part/pallas_call | solution.py:187
  237.4 12.1 %ref_part.4 = (f32[1280,1024]{1,0:T(8,128)}, f32[10,1,1024]{2,1,0:T(1,128)}, f32[10,1,1024]{2,1,0:T(1,128)}) custom-call(s32[1]{0:T(128)} %bitcast.core_ref, bf16[512,2560]{1,0:T(8,128)(2,1)} %q_ref.1, bf16[512,1280]{1,0:T(8,128)(2,1)} %collective-permute-done.qo_ref.q_ref, ...), custom_call_target="tpu_custom_call", output_to_operand_aliasing={{0}: (5, {}), {1}: (6, {}), {2}: (7, {})} | custom-call | flops 1342177280 | bytes 14417920 | tf_op jit(solution)/shard_map/ref_part/pallas_call | solution.py:187
  249.5 12.1 %ref_part.5 = (f32[1280,1024]{1,0:T(8,128)}, f32[10,1,1024]{2,1,0:T(1,128)}, f32[10,1,1024]{2,1,0:T(1,128)}) custom-call(s32[1]{0:T(128)} %bitcast.core_ref, bf16[512,2560]{1,0:T(8,128)(2,1)} %q_ref.1, bf16[512,1280]{1,0:T(8,128)(2,1)} %collective-permute-done.qo_ref.q_ref, ...), custom_call_target="tpu_custom_call", output_to_operand_aliasing={{0}: (5, {}), {1}: (6, {}), {2}: (7, {})} | custom-call | flops 1342177280 | bytes 14417920 | tf_op jit(solution)/shard_map/ref_part/pallas_call | solution.py:187
  261.6 0.7 copy-done.6
  262.4 9.5 %last_other.1 = bf16[512,1280]{1,0:T(8,128)(2,1)} custom-call(s32[1]{0:T(128)} %bitcast.core_ref, bf16[512,1280]{1,0:T(8,128)(2,1)} %collective-permute-done.qo_ref.q_ref, bf16[2,64,1280]{2,1,0:T(8,128)(2,1)} %copy-done.6, bf16[2,64,1280]{2,1,0:T(8,128)(2,1)} %copy-done.7, f32[1280,1024]{1,0:T(8,128)} %get-tuple-element.30.refs_2_, ...), custom_call_target="tpu_custom_call" | custom-call | flops 335544320 | bytes 5898240 | tf_op jit(solution)/shard_map/last_other/pallas_call | solution.py:232
  271.9 9.6 %last_own.1._ = bf16[512,2560]{1,0:T(8,128)(2,1)} custom-call(s32[1]{0:T(128)} %bitcast.core_ref, bf16[512,2560]{1,0:T(8,128)(2,1)} %q_ref.1, bf16[2,64,1280]{2,1,0:T(8,128)(2,1)} %copy-done.6, bf16[2,64,1280]{2,1,0:T(8,128)(2,1)} %copy-done.7, f32[1280,1024]{1,0:T(8,128)} %get-tuple-element.30.refs_2_, f32[10,1,1024]{2,1,0:T(1,128)} %get-tuple-element.31.refs_3_, ...), custom_call_target="tpu_custom_call" | custom-call | flops 335544320 | bytes 5898240 | tf_op jit(solution)/shard_map/last_own/pallas_call | solution.py:232
  281.5 1.1 copy-done.9
  282.6 3.5 %join_columns.1 = bf16[512,2560]{1,0:T(8,128)(2,1)} custom-call(s32[1]{0:T(128)} %bitcast.core_ref, bf16[512,1280]{1,0:T(8,128)(2,1)} %copy-done.9, bf16[512,2560]{1,0:T(8,128)(2,1)} %last_own.1._), custom_call_target="tpu_custom_call", output_to_operand_aliasing={{}: (2, {})} | custom-call | bytes 2621440 | tf_op jit(solution)/shard_map/join_columns/pallas_call | solution.py:261
  (58 shorter events, 1.9 us)
Async XLA Ops:
  0.0 14.1 %copy-start.12 = (s32[4]{0:T(128)S(1)}, s32[4]{0:T(128)}, u32[]{:S(2)}) copy-start(s32[4]{0:T(128)} %param.9) | copy-start | bytes 52
  0.0 14.1 %copy-start.13 = (s32[4]{0:T(128)S(1)}, s32[4]{0:T(128)}, u32[]{:S(2)}) copy-start(s32[4]{0:T(128)} %param.8) | copy-start | bytes 52
  13.6 20.9 %copy-start.1 = (bf16[2,512,1280]{2,1,0:T(8,128)(2,1)S(1)}, bf16[2,512,1280]{2,1,0:T(8,128)(2,1)}, u32[]{:S(2)}) copy-start(bf16[2,512,1280]{2,1,0:T(8,128)(2,1)} %get-tuple-element.19.mine) | copy-start | bytes 7864324
  13.6 5.4 %collective-permute-start.1 = (bf16[2,512,1280]{2,1,0:T(8,128)(2,1)}, bf16[2,512,1280]{2,1,0:T(8,128)(2,1)}, u32[]{:S(2)}, u32[]{:S(2)}) collective-permute-start(bf16[2,512,1280]{2,1,0:T(8,128)(2,1)} %get-tuple-element.20), channel_id=1, source_target_pairs={{0,1},{1,0},{2,3},{3,2},{4,5},{5,4},{6,7},{7,6},{8,9},{9,8},{10,11... | collective-permute-start | bytes 7864328 | tf_op jit(solution)/shard_map/ppermute | solution.py:294
  21.8 11.2 %collective-permute-start.2 = (bf16[2,64,1280]{2,1,0:T(8,128)(2,1)}, bf16[2,64,1280]{2,1,0:T(8,128)(2,1)}, u32[]{:S(2)}, u32[]{:S(2)}) collective-permute-start(bf16[2,64,1280]{2,1,0:T(8,128)(2,1)} %get-tuple-element.40), channel_id=1, source_target_pairs={{0,4},{4,8},{8,12},{12,14},{14,10},{10,6},{6,2},{2,0},{1,5},{5,9},... | collective-permute-start | bytes 983048 | tf_op jit(solution)/shard_map/ppermute | solution.py:349
  24.7 9.8 %collective-permute-start.6 = (bf16[2,64,1280]{2,1,0:T(8,128)(2,1)}, bf16[2,64,1280]{2,1,0:T(8,128)(2,1)}, u32[]{:S(2)}, u32[]{:S(2)}) collective-permute-start(bf16[2,64,1280]{2,1,0:T(8,128)(2,1)} %get-tuple-element.38), channel_id=1, source_target_pairs={{0,2},{4,0},{8,4},{12,8},{14,12},{10,14},{6,10},{2,6},{1,3},{5,1},... | collective-permute-start | bytes 983048 | tf_op jit(solution)/shard_map/ppermute | solution.py:350
  37.6 15.9 %collective-permute-start.7 = (bf16[2,128,1280]{2,1,0:T(8,128)(2,1)}, bf16[2,128,1280]{2,1,0:T(8,128)(2,1)}, u32[]{:S(2)}, u32[]{:S(2)}) collective-permute-start(bf16[2,128,1280]{2,1,0:T(8,128)(2,1)} %pad_maximum_fusion.1), channel_id=1, source_target_pairs={{0,2},{4,0},{8,4},{12,8},{14,12},{10,14},{6,10},{2,6},{1,3},{5,1},... | collective-permute-start | bytes 1966088 | tf_op jit(solution)/shard_map/ppermute | solution.py:350
  41.7 17.8 %collective-permute-start.3 = (bf16[2,128,1280]{2,1,0:T(8,128)(2,1)}, bf16[2,128,1280]{2,1,0:T(8,128)(2,1)}, u32[]{:S(2)}, u32[]{:S(2)}) collective-permute-start(bf16[2,128,1280]{2,1,0:T(8,128)(2,1)} %pad_maximum_fusion), channel_id=1, source_target_pairs={{0,4},{4,8},{8,12},{12,14},{14,10},{10,6},{6,2},{2,0},{1,5},{5,9},... | collective-permute-start | bytes 1966088 | tf_op jit(solution)/shard_map/ppermute | solution.py:349
  55.1 14.8 %collective-permute-start.8 = (bf16[2,128,1280]{2,1,0:T(8,128)(2,1)S(1)}, bf16[2,128,1280]{2,1,0:T(8,128)(2,1)}, u32[]{:S(2)}, u32[]{:S(2)}) collective-permute-start(bf16[2,128,1280]{2,1,0:T(8,128)(2,1)S(1)} %select_select_fusion.2), channel_id=1, source_target_pairs={{0,2},{4,0},{8,4},{12,8},{14,12},{10,14},{6,10},{2,6},{1,3},{5,1},... | collective-permute-start | bytes 1966088 | tf_op jit(solution)/shard_map/ppermute | solution.py:350
  73.2 18.5 %copy-start = (bf16[512,2560]{1,0:T(8,128)(2,1)S(1)}, bf16[512,2560]{1,0:T(8,128)(2,1)}, u32[]{:S(2)}) copy-start(bf16[512,2560]{1,0:T(8,128)(2,1)} %q_ref.1) | copy-start | bytes 7864324
  73.2 13.9 %collective-permute-start.4 = (bf16[2,128,1280]{2,1,0:T(8,128)(2,1)}, bf16[2,128,1280]{2,1,0:T(8,128)(2,1)}, u32[]{:S(2)}, u32[]{:S(2)}) collective-permute-start(bf16[2,128,1280]{2,1,0:T(8,128)(2,1)} %get-tuple-element.36), channel_id=1, source_target_pairs={{0,4},{4,8},{8,12},{12,14},{14,10},{10,6},{6,2},{2,0},{1,5},{5,9},... | collective-permute-start | bytes 1966088 | tf_op jit(solution)/shard_map/ppermute | solution.py:349
  76.7 16.2 %copy-start.14 = (s32[4,3]{1,0:T(4,128)S(1)}, s32[4,3]{1,0:T(4,128)}, u32[]{:S(2)}) copy-start(s32[4,3]{1,0:T(4,128)} %param.7) | copy-start | bytes 148
  76.7 19.9 %collective-permute-start.9 = (bf16[2,128,1280]{2,1,0:T(8,128)(2,1)}, bf16[2,128,1280]{2,1,0:T(8,128)(2,1)S(1)}, u32[]{:S(2)}, u32[]{:S(2)}) collective-permute-start(bf16[2,128,1280]{2,1,0:T(8,128)(2,1)} %get-tuple-element.35), channel_id=1, source_target_pairs={{0,2},{4,0},{8,4},{12,8},{14,12},{10,14},{6,10},{2,6},{1,3},{5,1},... | collective-permute-start | bytes 1966088 | tf_op jit(solution)/shard_map/ppermute | solution.py:350
  89.6 13.6 %collective-permute-start.5 = (bf16[2,128,1280]{2,1,0:T(8,128)(2,1)}, bf16[2,128,1280]{2,1,0:T(8,128)(2,1)}, u32[]{:S(2)}, u32[]{:S(2)}) collective-permute-start(bf16[2,128,1280]{2,1,0:T(8,128)(2,1)} %select_select_fusion.3), channel_id=1, source_target_pairs={{0,4},{4,8},{8,12},{12,14},{14,10},{10,6},{6,2},{2,0},{1,5},{5,9},... | collective-permute-start | bytes 1966088 | tf_op jit(solution)/shard_map/ppermute | solution.py:349
  92.9 14.2 %copy-start.2 = (bf16[2,512,1280]{2,1,0:T(8,128)(2,1)S(1)}, bf16[2,512,1280]{2,1,0:T(8,128)(2,1)}, u32[]{:S(2)}) copy-start(bf16[2,512,1280]{2,1,0:T(8,128)(2,1)} %get-tuple-element.19.mine) | copy-start | bytes 7864324
  92.9 100.1 %collective-permute-start = (bf16[512,1280]{1,0:T(8,128)(2,1)}, bf16[512,1280]{1,0:T(8,128)(2,1)}, u32[]{:S(2)}, u32[]{:S(2)}) collective-permute-start(bf16[512,1280]{1,0:T(8,128)(2,1)} %constant_dynamic-slice_fusion), channel_id=1, source_target_pairs={{0,1},{1,0},{2,3},{3,2},{4,5},{5,4},{6,7},{7,6},{8,9},{9,8},{10,11... | collective-permute-start | bytes 3932168 | tf_op jit(solution)/shard_map/ppermute | solution.py:295
  92.9 21.4 %collective-permute-start.18 = (s32[4,3]{1,0:T(4,128)S(1)}, s32[4,3]{1,0:T(4,128)S(1)}, u32[]{:S(2)}, u32[]{:S(2)}) collective-permute-start(s32[4,3]{1,0:T(4,128)S(1)} %copy-done.14), channel_id=1, source_target_pairs={{0,1},{1,0},{2,3},{3,2},{4,5},{5,4},{6,7},{7,6},{8,9},{9,8},{10,11... | collective-permute-start | bytes 152 | tf_op jit(solution)/shard_map/ppermute | solution.py:298
  105.0 5.5 %copy-start.3 = (bf16[2,128,1280]{2,1,0:T(8,128)(2,1)}, bf16[2,128,1280]{2,1,0:T(8,128)(2,1)S(1)}, u32[]{:S(2)}) copy-start(bf16[2,128,1280]{2,1,0:T(8,128)(2,1)S(1)} %select_select_fusion.refs_0_) | copy-start | bytes 1966084
  105.1 16.1 %collective-permute-start.10 = (bf16[2,128,1280]{2,1,0:T(8,128)(2,1)S(1)}, bf16[2,128,1280]{2,1,0:T(8,128)(2,1)S(1)}, u32[]{:S(2)}, u32[]{:S(2)}) collective-permute-start(bf16[2,128,1280]{2,1,0:T(8,128)(2,1)S(1)} %select_select_fusion.refs_0_), channel_id=1, source_target_pairs={{0,4},{4,8},{8,12},{12,14},{14,10},{10,6},{6,2},{2,0},{1,5},{5,9},... | collective-permute-start | bytes 1966088 | tf_op jit(solution)/shard_map/ppermute | solution.py:383
  107.0 42.9 %collective-permute-start.14 = (bf16[2,128,1280]{2,1,0:T(8,128)(2,1)S(1)}, bf16[2,128,1280]{2,1,0:T(8,128)(2,1)}, u32[]{:S(2)}, u32[]{:S(2)}) collective-permute-start(bf16[2,128,1280]{2,1,0:T(8,128)(2,1)S(1)} %select_select_fusion.refs_0_), channel_id=1, source_target_pairs={{0,2},{4,0},{8,4},{12,8},{14,12},{10,14},{6,10},{2,6},{1,3},{5,1},... | collective-permute-start | bytes 1966088 | tf_op jit(solution)/shard_map/ppermute | solution.py:384
  110.6 82.4 %collective-permute-start.19 = (bf16[2,256,1280]{2,1,0:T(8,128)(2,1)}, bf16[2,256,1280]{2,1,0:T(8,128)(2,1)S(1)}, u32[]{:S(2)}, u32[]{:S(2)}) collective-permute-start(bf16[2,256,1280]{2,1,0:T(8,128)(2,1)} %get-tuple-element.34), channel_id=1, source_target_pairs={{0,2},{1,3},{2,4},{3,5},{4,6},{5,7},{6,8},{7,9},{8,10},{9,11},{10,... | collective-permute-start | bytes 3932168 | tf_op jit(solution)/shard_map/ppermute | solution.py:360
  114.3 78.7 %collective-permute-start.20 = (bf16[2,256,1280]{2,1,0:T(8,128)(2,1)}, bf16[2,256,1280]{2,1,0:T(8,128)(2,1)}, u32[]{:S(2)}, u32[]{:S(2)}) collective-permute-start(bf16[2,256,1280]{2,1,0:T(8,128)(2,1)} %get-tuple-element.33), channel_id=1, source_target_pairs={{2,0},{3,1},{4,2},{5,3},{6,4},{7,5},{8,6},{9,7},{10,8},{11,9},{12,... | collective-permute-start | bytes 3932168 | tf_op jit(solution)/shard_map/ppermute | solution.py:361
  121.2 39.3 %copy-start.10 = (bf16[2,128,1280]{2,1,0:T(8,128)(2,1)}, bf16[2,128,1280]{2,1,0:T(8,128)(2,1)S(1)}, u32[]{:S(2)}) copy-start(bf16[2,128,1280]{2,1,0:T(8,128)(2,1)S(1)} %collective-permute-done.10.refs_1_) | copy-start | bytes 1966084
  121.2 39.3 %collective-permute-start.11 = (bf16[2,128,1280]{2,1,0:T(8,128)(2,1)S(1)}, bf16[2,128,1280]{2,1,0:T(8,128)(2,1)S(1)}, u32[]{:S(2)}, u32[]{:S(2)}) collective-permute-start(bf16[2,128,1280]{2,1,0:T(8,128)(2,1)S(1)} %collective-permute-done.10.refs_1_), channel_id=1, source_target_pairs={{0,4},{4,8},{8,12},{12,14},{14,10},{10,6},{6,2},{2,0},{1,5},{5,9},... | collective-permute-start | bytes 1966088 | tf_op jit(solution)/shard_map/ppermute | solution.py:383
  149.9 39.7 %collective-permute-start.15 = (bf16[2,128,1280]{2,1,0:T(8,128)(2,1)}, bf16[2,128,1280]{2,1,0:T(8,128)(2,1)}, u32[]{:S(2)}, u32[]{:S(2)}) collective-permute-start(bf16[2,128,1280]{2,1,0:T(8,128)(2,1)} %collective-permute-done.14.refs_2_), channel_id=1, source_target_pairs={{0,2},{4,0},{8,4},{12,8},{14,12},{10,14},{6,10},{2,6},{1,3},{5,1},... | collective-permute-start | bytes 1966088 | tf_op jit(solution)/shard_map/ppermute | solution.py:384
  160.5 61.5 %copy-start.11 = (bf16[2,128,1280]{2,1,0:T(8,128)(2,1)}, bf16[2,128,1280]{2,1,0:T(8,128)(2,1)S(1)}, u32[]{:S(2)}) copy-start(bf16[2,128,1280]{2,1,0:T(8,128)(2,1)S(1)} %collective-permute-done.11.refs_0_) | copy-start | bytes 1966084
  160.5 61.5 %collective-permute-start.12 = (bf16[2,128,1280]{2,1,0:T(8,128)(2,1)S(1)}, bf16[2,128,1280]{2,1,0:T(8,128)(2,1)S(1)}, u32[]{:S(2)}, u32[]{:S(2)}) collective-permute-start(bf16[2,128,1280]{2,1,0:T(8,128)(2,1)S(1)} %collective-permute-done.11.refs_0_), channel_id=1, source_target_pairs={{0,4},{4,8},{8,12},{12,14},{14,10},{10,6},{6,2},{2,0},{1,5},{5,9},... | collective-permute-start | bytes 1966088 | tf_op jit(solution)/shard_map/ppermute | solution.py:383
  189.6 32.5 %collective-permute-start.16 = (bf16[2,128,1280]{2,1,0:T(8,128)(2,1)}, bf16[2,128,1280]{2,1,0:T(8,128)(2,1)S(1)}, u32[]{:S(2)}, u32[]{:S(2)}) collective-permute-start(bf16[2,128,1280]{2,1,0:T(8,128)(2,1)} %collective-permute-done.15.refs_1_), channel_id=1, source_target_pairs={{0,2},{4,0},{8,4},{12,8},{14,12},{10,14},{6,10},{2,6},{1,3},{5,1},... | collective-permute-start | bytes 1966088 | tf_op jit(solution)/shard_map/ppermute | solution.py:384
  193.0 1.1 copy-start.8
  222.0 15.4 %copy-start.4 = (bf16[2,128,1280]{2,1,0:T(8,128)(2,1)}, bf16[2,128,1280]{2,1,0:T(8,128)(2,1)S(1)}, u32[]{:S(2)}) copy-start(bf16[2,128,1280]{2,1,0:T(8,128)(2,1)S(1)} %collective-permute-done.12.refs_0_) | copy-start | bytes 1966084
  222.0 39.5 %collective-permute-start.13 = (bf16[2,64,1280]{2,1,0:T(8,128)(2,1)S(1)}, bf16[2,64,1280]{2,1,0:T(8,128)(2,1)S(1)}, u32[]{:S(2)}, u32[]{:S(2)}) collective-permute-start(bf16[2,64,1280]{2,1,0:T(8,128)(2,1)S(1)} %slice.24), channel_id=1, source_target_pairs={{0,4},{4,8},{8,12},{12,14},{14,10},{10,6},{6,2},{2,0},{1,5},{5,9},... | collective-permute-start | bytes 983048 | tf_op jit(solution)/shard_map/ppermute | solution.py:383
  222.1 15.3 %copy-start.5 = (bf16[2,128,1280]{2,1,0:T(8,128)(2,1)}, bf16[2,128,1280]{2,1,0:T(8,128)(2,1)S(1)}, u32[]{:S(2)}) copy-start(bf16[2,128,1280]{2,1,0:T(8,128)(2,1)S(1)} %collective-permute-done.16.refs_1_) | copy-start | bytes 1966084
  222.2 39.4 %collective-permute-start.17 = (bf16[2,64,1280]{2,1,0:T(8,128)(2,1)S(1)}, bf16[2,64,1280]{2,1,0:T(8,128)(2,1)S(1)}, u32[]{:S(2)}, u32[]{:S(2)}) collective-permute-start(bf16[2,64,1280]{2,1,0:T(8,128)(2,1)S(1)} %slice.25), channel_id=1, source_target_pairs={{0,2},{4,0},{8,4},{12,8},{14,12},{10,14},{6,10},{2,6},{1,3},{5,1},... | collective-permute-start | bytes 983048 | tf_op jit(solution)/shard_map/ppermute | solution.py:384
  261.5 0.7 copy-start.6
  261.6 0.8 copy-start.7
  271.9 9.6 %collective-permute-start.21 = (bf16[512,1280]{1,0:T(8,128)(2,1)}, bf16[512,1280]{1,0:T(8,128)(2,1)S(1)}, u32[]{:S(2)}, u32[]{:S(2)}) collective-permute-start(bf16[512,1280]{1,0:T(8,128)(2,1)} %last_other.1), channel_id=1, source_target_pairs={{0,1},{1,0},{2,3},{3,2},{4,5},{5,4},{6,7},{7,6},{8,9},{9,8},{10,11... | collective-permute-start | bytes 3932168 | tf_op jit(solution)/shard_map/ppermute | solution.py:391
  281.4 1.1 copy-start.9
